TPU v7x, 32 devices: a whole 2x2x4 slice. The times are simulated.
32 devices in a mesh: box: 4 (over z), row: 4 (over y, core), col: 2 (over x).
Axes of the slice: x: 2, y: 2, z: 4, core: 2. Of those that a mesh axis runs over, the one named last changes fastest.
Arguments:
- ext_ext: float32 [4, 3072, 3072], P('box', 'row', 'col'), may hold values from -6 to 6
- ext_int: float32 [4, 3072, 1024], P('box', 'row', 'col'), may hold values from -0.1875 to 0.1875
- int_ext: float32 [4, 1024, 3072], P('box', 'row', 'col'), may hold values from -6 to 6
- int_int: float32 [4, 1024, 1024], P('box', 'row', 'col'), may hold values from -0.1 to 0.1, as said below
Outputs:
- merged: float32 [4, 3072, 2, 3072], P('box', 'row', None, 'col')
Inputs may be any that keep to these rules, and one draw needn't show every extreme that they name: `int_int`: independent entries.
All inputs are finite; a program needn't handle non-finite values.
Results may differ from a plain program's by a relative error of at most 0.0003.
Values sent between devices are 32-bit elements; how exact they have to be, the bound alone decides.
No kernel may reach another device: no remote copies, remote signals or barrier semaphores. Data moves between devices by JAX's collectives and lax.ppermute only.
A program may use at most 128 MiB of HBM per device.

v0:
```python
import jax
import jax.numpy as jnp
from jax import lax
from jax.sharding import PartitionSpec as P

HIGH = lax.Precision.HIGHEST


def swapped(shard, axis, distance):
    return lax.ppermute(shard, axis, [(i, i ^ 1 << distance) for i in range(lax.axis_size(axis))])


def panel_dot(total, piece, panel):
    return total + jnp.dot(piece, panel, precision=HIGH, preferred_element_type=jnp.float32)


def chain_product(left, right):
    panel = lax.all_gather(right, "row", axis=0, tiled=True)
    empty = jnp.zeros((left.shape[0], right.shape[1]), jnp.float32)
    return panel_dot(empty, lax.all_gather(left, "col", axis=1, tiled=True), panel)


def local(ext_ext, ext_int, int_ext, int_int):
    own_ee = ext_ext[0]
    own_ed = ext_int[0]
    own_de = int_ext[0]
    own_dd = int_int[0]
    partner_dd, partner_de = swapped((own_dd, own_de), "box", 0)
    is_even = lax.axis_index("box") % 2 == 0
    block_rows = own_dd.shape[0]
    block_cols = own_dd.shape[1]
    row_ids = lax.axis_index("row") * block_rows + lax.broadcasted_iota(
        jnp.int32, (block_rows, block_cols), 0
    )
    col_ids = lax.axis_index("col") * block_cols + lax.broadcasted_iota(
        jnp.int32, (block_rows, block_cols), 1
    )
    identity = (row_ids == col_ids).astype(jnp.float32)
    coupling = chain_product(partner_dd, own_dd)
    square = chain_product(coupling, coupling)
    first = identity + coupling
    inverse = first + chain_product(first, square)
    de_panel = lax.all_gather(own_de, "row", axis=0, tiled=True)
    coupled = panel_dot(
        jnp.zeros(own_de.shape, jnp.float32),
        lax.all_gather(partner_dd, "col", axis=1, tiled=True),
        de_panel,
    )
    source = jnp.concatenate(
        [jnp.where(is_even, coupled, partner_de), jnp.where(is_even, partner_de, coupled)], axis=1
    )
    source_panel = lax.all_gather(source, "row", axis=0, tiled=True)
    pieces = lax.all_gather(inverse[None], ("row", "col"), axis=0, tiled=True)
    row_count = lax.axis_size("row")
    col_count = lax.axis_size("col")
    whole = pieces.reshape(row_count, col_count, block_rows, block_cols).transpose(0, 2, 1, 3)
    whole = whole.reshape(row_count * block_rows, col_count * block_cols)
    right_panel = jnp.dot(whole, source_panel, precision=HIGH, preferred_element_type=jnp.float32)
    zeros = jnp.zeros_like(own_ee)
    start_terms = jnp.concatenate(
        [jnp.where(is_even, own_ee, zeros), jnp.where(is_even, zeros, own_ee)], axis=1
    )
    merged = panel_dot(start_terms, lax.all_gather(own_ed, "col", axis=1, tiled=True), right_panel)
    return merged.reshape(1, own_ee.shape[0], 2, own_ee.shape[1])


def solution(mesh):
    placed = (
        P("box", "row", "col"),
        P("box", "row", "col"),
        P("box", "row", "col"),
        P("box", "row", "col"),
    )
    return jax.shard_map(
        local, mesh=mesh, in_specs=placed, out_specs=P("box", "row", None, "col"), check_vma=False
    )
```

profile of v0, /device:TPU:0, one launch (start us, length us, event | category | flops | bytes accessed | tf_op | source)
XLA Modules:
  0.0 469.0 jit_solution(2206762846612566274)
XLA Ops:
  6.5 0.0 all-gather.15.cloned.1.call-start
  6.5 3.1 collective-permute-start
  9.6 12.1 %collective-permute-done = f32[256,512]{1,0:T(8,128)S(1)} collective-permute-done((f32[256,512]{1,0:T(8,128)}, f32[256,512]{1,0:T(8,128)S(1)}, u32[]{:S(2)}, u32[]{:S(2)}) %collective-permute-start) | collective-permute-done | bytes 524320 | tf_op jit(solution)/shard_map/ppermute | solution.py:10
  21.7 0.8 copy-done.2
  22.5 0.0 all-gather.15.cloned.1.call-update
  22.5 0.0 all-gather.27.cloned.1.call-start
  22.6 0.7 all-gather.27.cloned.1.call-update
  23.3 0.0 all-gather.19.cloned.1.call-start
  23.4 22.0 %all-gather.15.cloned.1.call-done = f32[256,1024]{1,0:T(8,128)} async-done(((f32[256,512]{1,0:T(8,128)}), f32[256,1024]{1,0:T(8,128)}) %all-gather.15.cloned.1.call-update) | async-done | bytes 1048592 | tf_op jit(solution)/shard_map/all_gather | solution.py:20
  45.4 24.2 %all-gather.27.cloned.1.call-done = f32[1,1024,512]{2,1,0:T(8,128)} async-done(((f32[1,256,512]{2,1,0:T(8,128)}), f32[1,1024,512]{2,1,0:T(8,128)}) %all-gather.27.cloned.1.call-update) | async-done | bytes 2097168 | tf_op jit(solution)/shard_map/all_gather | solution.py:18
  69.5 4.8 %convert_add_fusion = (f32[256,512]{1,0:T(8,128)}, f32[256,512]{1,0:T(8,128)}) fusion(s32[512]{0:T(512)S(1)} %iota_add_fusion, s32[256]{0:T(256)S(1)} %iota_add_fusion.1, f32[256,1024]{1,0:T(8,128)} %all-gather.15.cloned.1.call-done, f32[1,1024,512]{2,1,0:T(8,128)} %all-gather.27.cloned.1.call-done), kind=kOutput, calls=%fused_computation.12 | convolution fusion | flops 1611005952 | bytes 4197376 | tf_op jit(solution)/shard_map/dot_general | solution.py:14
  74.4 0.0 all-gather.19.cloned.1.call-update
  74.4 0.0 all-gather.21.cloned.1.call-start
  74.4 0.5 all-gather.21.cloned.1.call-update
  75.0 0.0 all-gather.17.cloned.1.call-start
  75.0 0.5 all-gather.17.cloned.1.call-update
  75.6 0.0 all-gather.23.cloned.1.call-start
  75.6 20.2 %all-gather.19.cloned.1.call-done = f32[256,1024]{1,0:T(8,128)} async-done(((f32[256,512]{1,0:T(8,128)}), f32[256,1024]{1,0:T(8,128)}) %all-gather.19.cloned.1.call-update) | async-done | bytes 1048592 | tf_op jit(solution)/shard_map/all_gather | solution.py:20
  95.8 24.0 %all-gather.21.cloned.1.call-done = f32[1024,512]{1,0:T(8,128)} async-done(((f32[256,512]{1,0:T(8,128)}), f32[1024,512]{1,0:T(8,128)}) %all-gather.21.cloned.1.call-update) | async-done | bytes 2097168 | tf_op jit(solution)/shard_map/all_gather | solution.py:18
  119.8 4.6 fusion.5
  124.5 0.0 all-gather.23.cloned.1.call-update
  124.5 0.0 all-gather.31.cloned.1.call-start
  124.6 0.7 all-gather.31.cloned.1.call-update
  125.3 0.0 all-gather.29.cloned.1.call-start
  125.3 17.2 %all-gather.17.cloned.1.call-done = f32[256,1024]{1,0:T(8,128)} async-done(((f32[256,512]{1,0:T(8,128)}), f32[256,1024]{1,0:T(8,128)}) %all-gather.17.cloned.1.call-update) | async-done | bytes 1048592 | tf_op jit(solution)/shard_map/all_gather | solution.py:20
  142.5 24.0 %all-gather.23.cloned.1.call-done = f32[1024,512]{1,0:T(8,128)} async-done(((f32[256,512]{1,0:T(8,128)}), f32[1024,512]{1,0:T(8,128)}) %all-gather.23.cloned.1.call-update) | async-done | bytes 2097168 | tf_op jit(solution)/shard_map/all_gather | solution.py:18
  166.6 0.0 copy-done
  166.6 4.6 convolution_add_fusion
  171.2 0.0 all-gather.29.cloned.1.call-update
  171.2 0.0 all-gather.25.cloned.1.call-start
  171.3 1.6 collective-permute-start.1
  172.8 35.3 %collective-permute-done.1 = f32[256,1536]{1,0:T(8,128)S(1)} collective-permute-done((f32[256,1536]{1,0:T(8,128)}, f32[256,1536]{1,0:T(8,128)S(1)}, u32[]{:S(2)}, u32[]{:S(2)}) %collective-permute-start.1) | collective-permute-done | bytes 1572896 | tf_op jit(solution)/shard_map/ppermute | solution.py:10
  208.1 6.4 %all-gather.31.cloned.1.call-done = f32[1,1024,1536]{2,1,0:T(8,128)} async-done(((f32[1,256,1536]{2,1,0:T(8,128)}), f32[1,1024,1536]{2,1,0:T(8,128)}) %all-gather.31.cloned.1.call-update) | async-done | bytes 6291472 | tf_op jit(solution)/shard_map/all_gather | solution.py:43
  214.5 7.6 %broadcast_select_fusion.1 = (f32[256,1536]{1,0:T(8,128)S(1)}, f32[256,1536]{1,0:T(8,128)S(1)}) fusion(f32[256,1536]{1,0:T(8,128)S(1)} %collective-permute-done.1, pred[]{:T(512)S(6)} %eq.8, f32[256,1024]{1,0:T(8,128)S(1)} %copy-done.1, f32[1,1024,1536]{2,1,0:T(8,128)} %all-gather.31.cloned.1.call-done), kind=kOutput, calls=%fused_computation.11 | convolution fusion | flops 4832624640 | bytes 12058625 | tf_op jit(solution)/shard_map/dot_general | solution.py:14
  222.1 1.9 pad_maximum_fusion
  224.1 0.0 all-gather.25.cloned.1.call-update
  224.1 0.2 all-gather.33.cloned.1.call-start
  224.3 0.4 all-gather.33.cloned.1.call-update
  224.7 6.1 %copy.8 = f32[1,768,1536]{1,2,0:T(8,128)} copy(f32[1,768,1536]{2,1,0:T(8,128)} %param.4) | data formatting | bytes 9437184 | tf_op args[0]
  230.7 6.7 %select_bitcast_fusion.1 = (f32[768,1536]{0,1:T(8,128)}, f32[768,1536]{0,1:T(8,128)}) fusion(f32[1,768,1536]{1,2,0:T(8,128)} %copy.8, pred[]{:T(512)S(6)} %eq.8), kind=kLoop, calls=%fused_computation.4 | loop fusion | flops 2359296 | bytes 14155777 | tf_op jit(solution)/shard_map/jit(_where)/select_n | solution.py:61
  237.4 15.6 %all-gather.29.cloned.1.call-done = f32[2048,512]{1,0:T(8,128)} async-done(((f32[256,512]{1,0:T(8,128)}), f32[2048,512]{1,0:T(8,128)}) %all-gather.29.cloned.1.call-update) | async-done | bytes 4194320 | tf_op jit(solution)/shard_map/all_gather | solution.py:53
  253.0 5.4 %copy.10 = f32[4,2,256,512]{3,1,2,0:T(2,128)S(1)} copy(f32[4,2,256,512]{3,2,1,0:T(8,128)} %bitcast.38) | data formatting | bytes 8388608 | tf_op jit(solution)/shard_map/reshape | solution.py:56
  258.4 3.1 copy.12
  261.5 75.2 %all-gather.25.cloned.1.call-done = f32[1024,3072]{1,0:T(8,128)} async-done(((f32[256,3072]{1,0:T(8,128)}), f32[1024,3072]{1,0:T(8,128)}) %all-gather.25.cloned.1.call-update) | async-done | bytes 12582928 | tf_op jit(solution)/shard_map/all_gather | solution.py:52
  336.7 44.8 %fusion.6 = f32[1024,3072]{1,0:T(8,128)} fusion(f32[1024,1024]{1,0:T(8,128)} %bitcast.39, f32[1024,3072]{1,0:T(8,128)} %all-gather.25.cloned.1.call-done), kind=kOutput, calls=%fused_computation.16 | convolution fusion | flops 38654705664 | bytes 29360128 | tf_op jit(solution)/shard_map/dot_general | solution.py:58
  381.4 1.6 all-gather.33.cloned.1.call-done
  383.0 64.4 %maximum_add_fusion = f32[768,3072]{0,1:T(8,128)} fusion(f32[768,1536]{0,1:T(8,128)} %get-tuple-element.6, f32[768,1536]{0,1:T(8,128)} %get-tuple-element.5, f32[1024,3072]{1,0:T(8,128)} %fusion.6, f32[1,768,1024]{2,1,0:T(8,128)} %all-gather.33.cloned.1.call-done), kind=kOutput, calls=%fused_computation | convolution fusion | flops 28995747840 | bytes 34603008 | tf_op jit(solution)/shard_map/dot_general | solution.py:14
  447.4 14.8 %copy.11 = f32[1,768,2,1536]{3,2,1,0:T(2,128)} copy(f32[1,768,2,1536]{1,3,2,0:T(8,128)} %bitcast.37) | data formatting | bytes 18874368 | tf_op jit(solution)/shard_map/reshape | solution.py:64
  (6 shorter events, 0.0 us)
Async XLA Ops:
  6.5 38.9 %all-gather.15.cloned.1.call-start = ((), (), s32[]{:S(2)}) async-start(), calls=%async_computation | async-start | bytes 1572864 | tf_op jit(solution)/shard_map/all_gather | solution.py:20
  6.5 15.2 %collective-permute-start = (f32[256,512]{1,0:T(8,128)}, f32[256,512]{1,0:T(8,128)S(1)}, u32[]{:S(2)}, u32[]{:S(2)}) collective-permute-start(f32[256,512]{1,0:T(8,128)} %bitcast.41), channel_id=1, source_target_pairs={{0,8},{8,0},{16,24},{24,16},{1,9},{9,1},{17,25},{25,17},{2,10},{10... | collective-permute-start | bytes 1572872 | tf_op jit(solution)/shard_map/ppermute | solution.py:10
  21.7 0.8 copy-start.2
  22.5 47.0 %all-gather.27.cloned.1.call-start = ((), (), s32[]{:S(2)}) async-start(), calls=%async_computation.6 | async-start | bytes 2621440 | tf_op jit(solution)/shard_map/all_gather | solution.py:18
  23.3 72.5 %all-gather.19.cloned.1.call-start = ((), (), s32[]{:S(2)}) async-start(), calls=%async_computation.2 | async-start | bytes 1572864 | tf_op jit(solution)/shard_map/all_gather | solution.py:20
  74.4 92.2 %copy-start = (f32[256,512]{1,0:T(8,128)S(1)}, f32[256,512]{1,0:T(8,128)}, u32[]{:S(2)}) copy-start(f32[256,512]{1,0:T(8,128)} %get-tuple-element.9) | copy-start | bytes 1572868
  74.4 45.4 %all-gather.21.cloned.1.call-start = ((), (), s32[]{:S(2)}) async-start(), calls=%async_computation.3 | async-start | bytes 2621440 | tf_op jit(solution)/shard_map/all_gather | solution.py:18
  75.0 67.6 %all-gather.17.cloned.1.call-start = ((), (), s32[]{:S(2)}) async-start(), calls=%async_computation.1 | async-start | bytes 1572864 | tf_op jit(solution)/shard_map/all_gather | solution.py:20
  75.6 91.0 %all-gather.23.cloned.1.call-start = ((), (), s32[]{:S(2)}) async-start(), calls=%async_computation.4 | async-start | bytes 2621440 | tf_op jit(solution)/shard_map/all_gather | solution.py:18
  124.5 90.0 %copy-start.1 = (f32[256,1024]{1,0:T(8,128)S(1)}, f32[256,1024]{1,0:T(8,128)}, u32[]{:S(2)}) copy-start(f32[256,1024]{1,0:T(8,128)} %all-gather.15.cloned.1.call-done) | copy-start | bytes 3145732
  124.5 90.0 %all-gather.31.cloned.1.call-start = ((), (), s32[]{:S(2)}) async-start(), calls=%async_computation.8 | async-start | bytes 7864320 | tf_op jit(solution)/shard_map/all_gather | solution.py:43
  125.3 127.7 %all-gather.29.cloned.1.call-start = ((), (), s32[]{:S(2)}) async-start(), calls=%async_computation.7 | async-start | bytes 4718592 | tf_op jit(solution)/shard_map/all_gather | solution.py:53
  171.2 165.5 %all-gather.25.cloned.1.call-start = ((), (), s32[]{:S(2)}) async-start(), calls=%async_computation.5 | async-start | bytes 15728640 | tf_op jit(solution)/shard_map/all_gather | solution.py:52
  171.3 36.8 %collective-permute-start.1 = (f32[256,1536]{1,0:T(8,128)}, f32[256,1536]{1,0:T(8,128)S(1)}, u32[]{:S(2)}, u32[]{:S(2)}) collective-permute-start(f32[256,1536]{1,0:T(8,128)} %bitcast.40), channel_id=1, source_target_pairs={{0,8},{8,0},{16,24},{24,16},{1,9},{9,1},{17,25},{25,17},{2,10},{10... | collective-permute-start | bytes 4718600 | tf_op jit(solution)/shard_map/ppermute | solution.py:10
  224.1 158.9 %all-gather.33.cloned.1.call-start = ((), (), s32[]{:S(2)}) async-start(), calls=%async_computation.9 | async-start | bytes 4718592 | tf_op jit(solution)/shard_map/all_gather | solution.py:63
Sparse Core Ops, SparseCore 0:
  22.7 22.6 all-gather.14
  46.9 22.5 all-gather.26
  74.5 21.2 all-gather.18
  97.2 22.5 all-gather.20
  121.2 21.2 all-gather.16
  143.9 22.5 all-gather.22
  168.1 46.3 all-gather.30
  216.4 36.5 all-gather.28
  254.6 82.0 all-gather.24
  338.1 44.8 all-gather.32
where the time goes:
time: 470 us; the launch traced here: 469 us
  waiting for transfers between devices  281 us (60%)
  matrix products  131 us (28%)
  local copies, waits for them, and re-layouts  30.1 us (6%)
  between operations  13.6 us (3%)
  other arithmetic  8.65 us (2%)
  starting transfers between devices  5.14 us (1%)
    dot_general x5, matrix products, panel_dot(): jnp.dot(piece, panel, precision=HIGH, preferred_element_type=jnp.float32)  86.1 us
    all_gather x1, waiting for transfers between devices, local(): source_panel = lax.all_gather(source, 'row', axis=0, tiled=True)  75.2 us
    all_gather x3, waiting for transfers between devices, chain_product(): panel = lax.all_gather(right, 'row', axis=0, tiled=True)  72.2 us
    all_gather x3, waiting for transfers between devices, chain_product(): lax.all_gather(left, 'col', axis=1, tiled=True)  59.5 us
    ppermute x2, waiting for transfers between devices, swapped(): lax.ppermute(shard, axis, [(i, i ^ 1 << distance) for i in range(lax.axis...  47.4 us
    dot_general x1, matrix products, local(): jnp.dot(whole, source_panel, precision=HIGH, preferred_element_type=jnp.f...  44.8 us
    all_gather x1, waiting for transfers between devices, local(): pieces = lax.all_gather(inverse[None], ('row', 'col'), axis=0, tiled=True)  15.6 us
    reshape x1, local copies, waits for them, and re-layouts, local(): return merged.reshape(1, own_ee.shape[0], 2, own_ee.shape[1])  14.8 us
  transfers between devices with their start and end apart: 12, of which 12 were waited for; matrix products, arithmetic and copies ran while one was open for 18% of the time, Pallas kernels for 0%

commit v1 on v0

--- a/solution.py
+++ b/solution.py
@@ -15,7 +15,12 @@
 
 
 def chain_product(left, right):
-    panel = lax.all_gather(right, "row", axis=0, tiled=True)
+    ring = [right]
+    for hop in range(3):
+        ring.append(lax.ppermute(ring[-1], "row", [(dev, (dev + 1) % 4) for dev in range(4)]))
+    panel = jnp.roll(
+        jnp.concatenate(ring[::-1], axis=0), (lax.axis_index("row") + 1) * ring[0].shape[0], axis=0
+    )
     empty = jnp.zeros((left.shape[0], right.shape[1]), jnp.float32)
     return panel_dot(empty, lax.all_gather(left, "col", axis=1, tiled=True), panel)
 

time: 470 us -> 407 us (0.87); the launches traced: 469 us -> 399 us
  waiting for transfers between devices: 281 us -> 209 us
    all_gather x3 -> x0, waiting for transfers between devices: 72.2 us -> none  [chain_product(): panel = lax.all_gather(right, 'row', axis=0, tiled=True)]
    ppermute x0 -> x9, waiting for transfers between devices: none -> 60.6 us  [chain_product(): lax.ppermute(ring[-1], 'row', [(dev, (dev + 1) % 4) for dev in range(4)])]
    all_gather x3, waiting for transfers between devices: 59.5 us -> 16.7 us  [chain_product(): lax.all_gather(left, 'col', axis=1, tiled=True)]
    all_gather x1, waiting for transfers between devices: 15.6 us -> 5.26 us  [local(): pieces = lax.all_gather(inverse[None], ('row', 'col'), axis=0, tiled=True)]
    all_gather x1, waiting for transfers between devices: 6.43 us -> 0.01 us  [local(): de_panel = lax.all_gather(own_de, 'row', axis=0, tiled=True)]
  transfers between devices with their start and end apart: 12 -> 18, of which waited for: 12 -> 14; matrix products, arithmetic and copies ran while one was open for 18% -> 21% of each run, Pallas kernels for 0% -> 0%
where the time goes in v1:
time: 407 us; the launch traced here: 399 us
  waiting for transfers between devices  209 us (51%)
  matrix products  132 us (32%)
  local copies, waits for them, and re-layouts  30.2 us (7%)
  between operations  14 us (3%)
  other arithmetic  8.67 us (2%)
  starting transfers between devices  5.14 us (1%)
    dot_general x5, matrix products, panel_dot(): jnp.dot(piece, panel, precision=HIGH, preferred_element_type=jnp.float32)  87.6 us
    all_gather x1, waiting for transfers between devices, local(): source_panel = lax.all_gather(source, 'row', axis=0, tiled=True)  75 us
    ppermute x9, waiting for transfers between devices, chain_product(): lax.ppermute(ring[-1], 'row', [(dev, (dev + 1) % 4) for dev in range(4)])  60.6 us
    ppermute x2, waiting for transfers between devices, swapped(): lax.ppermute(shard, axis, [(i, i ^ 1 << distance) for i in range(lax.axis...  47.5 us
    dot_general x1, matrix products, local(): jnp.dot(whole, source_panel, precision=HIGH, preferred_element_type=jnp.f...  44.8 us
    all_gather x3, waiting for transfers between devices, chain_product(): lax.all_gather(left, 'col', axis=1, tiled=True)  16.7 us
    reshape x1, local copies, waits for them, and re-layouts, local(): return merged.reshape(1, own_ee.shape[0], 2, own_ee.shape[1])  14.8 us
    unnamed x8, local copies, waits for them, and re-layouts  10 us
  transfers between devices with their start and end apart: 18, of which 14 were waited for; matrix products, arithmetic and copies ran while one was open for 21% of the time, Pallas kernels for 0%

profile of v1, /device:TPU:0, one launch (start us, length us, event | category | flops | bytes accessed | tf_op | source)
XLA Modules:
  0.0 399.1 jit_solution(3581380616287302409)
XLA Ops:
  6.5 3.1 collective-permute-start.3
  9.6 0.0 collective-permute-start
  9.6 12.1 %collective-permute-done.3 = f32[256,512]{1,0:T(8,128)S(1)} collective-permute-done((f32[256,512]{1,0:T(8,128)}, f32[256,512]{1,0:T(8,128)S(1)}, u32[]{:S(2)}, u32[]{:S(2)}) %collective-permute-start.3) | collective-permute-done | bytes 524320 | tf_op jit(solution)/shard_map/ppermute | solution.py:10
  21.7 0.8 copy-done.2
  22.5 0.0 all-gather.11.cloned.1.call-update
  22.5 0.0 all-gather.15.cloned.1.call-start
  22.6 0.1 collective-permute-start.1
  22.7 8.6 %collective-permute-done.1 = f32[256,512]{1,0:T(8,128)S(1)} collective-permute-done((f32[256,512]{1,0:T(8,128)S(1)}, f32[256,512]{1,0:T(8,128)S(1)}, u32[]{:S(2)}, u32[]{:S(2)}) %collective-permute-start.1) | collective-permute-done | bytes 524320 | tf_op jit(solution)/shard_map/ppermute | solution.py:20
  31.3 14.1 %all-gather.11.cloned.1.call-done = f32[256,1024]{1,0:T(8,128)} async-done(((f32[256,512]{1,0:T(8,128)}), f32[256,1024]{1,0:T(8,128)}) %all-gather.11.cloned.1.call-update) | async-done | bytes 1048592 | tf_op jit(solution)/shard_map/all_gather | solution.py:25
  45.4 5.4 %convert_add_fusion = (f32[256,512]{1,0:T(8,128)}, f32[256,512]{1,0:T(8,128)}) fusion(s32[512]{0:T(512)S(1)} %iota_add_fusion, s32[256]{0:T(256)S(1)} %iota_add_fusion.1, f32[256,1024]{1,0:T(8,128)} %all-gather.11.cloned.1.call-done, s32[]{:T(128)S(6)} %select_n.60, f32[256,512]{1,0:T(8,128)S(1)} %collective-permute-done.2, ...), kind=kOutput, calls=%fused_computation.59 | convolution fusion | flops 1614675968 | bytes 4197380 | tf_op jit(solution)/shard_map/dot_general | solution.py:14
  50.8 0.0 all-gather.15.cloned.1.call-update
  50.8 0.0 all-gather.13.cloned.1.call-start
  50.9 0.7 all-gather.13.cloned.1.call-update
  51.5 0.0 all-gather.21.cloned.1.call-start
  51.6 0.5 all-gather.21.cloned.1.call-update
  52.1 0.0 copy-start.1
  52.1 0.0 all-gather.19.cloned.1.call-start
  52.2 0.1 collective-permute-start.4
  52.2 8.8 %collective-permute-done.4 = f32[256,512]{1,0:T(8,128)S(1)} collective-permute-done((f32[256,512]{1,0:T(8,128)}, f32[256,512]{1,0:T(8,128)S(1)}, u32[]{:S(2)}, u32[]{:S(2)}) %collective-permute-start.4) | collective-permute-done | bytes 524320 | tf_op jit(solution)/shard_map/ppermute | solution.py:20
  61.1 8.6 %collective-permute-done.5 = f32[256,512]{1,0:T(8,128)S(1)} collective-permute-done((f32[256,512]{1,0:T(8,128)S(1)}, f32[256,512]{1,0:T(8,128)S(1)}, u32[]{:S(2)}, u32[]{:S(2)}) %collective-permute-start.5) | collective-permute-done | bytes 524320 | tf_op jit(solution)/shard_map/ppermute | solution.py:20
  69.7 2.6 all-gather.15.cloned.1.call-done
  72.2 6.0 %collective-permute-done.6 = f32[256,512]{1,0:T(8,128)S(1)} collective-permute-done((f32[256,512]{1,0:T(8,128)S(1)}, f32[256,512]{1,0:T(8,128)S(1)}, u32[]{:S(2)}, u32[]{:S(2)}) %collective-permute-start.6) | collective-permute-done | bytes 524320 | tf_op jit(solution)/shard_map/ppermute | solution.py:20
  78.3 4.3 %fusion.17 = f32[256,512]{1,0:T(8,128)S(1)} fusion(f32[256,1024]{1,0:T(8,128)} %all-gather.15.cloned.1.call-done, s32[]{:T(128)S(6)} %select_n.60, f32[256,512]{1,0:T(8,128)S(1)} %collective-permute-done.6, f32[256,512]{1,0:T(8,128)S(1)} %collective-permute-done.5, f32[256,512]{1,0:T(8,128)S(1)} %collective-permute-done.4, f32[256,512]{1,0:T(8,128)} %get-tuple-element.11), kind=kOutput, calls=%fused_computation.43 | convolution fusion | flops 1614282752 | bytes 3670020 | tf_op jit(solution)/shard_map/dot_general | solution.py:14
  82.6 0.0 copy-start
  82.6 0.1 collective-permute-start.7
  82.7 8.6 %collective-permute-done.7 = f32[256,512]{1,0:T(8,128)S(1)} collective-permute-done((f32[256,512]{1,0:T(8,128)S(1)}, f32[256,512]{1,0:T(8,128)S(1)}, u32[]{:S(2)}, u32[]{:S(2)}) %collective-permute-start.7) | collective-permute-done | bytes 524320 | tf_op jit(solution)/shard_map/ppermute | solution.py:20
  91.3 8.7 %collective-permute-done.8 = f32[256,512]{1,0:T(8,128)} collective-permute-done((f32[256,512]{1,0:T(8,128)S(1)}, f32[256,512]{1,0:T(8,128)}, u32[]{:S(2)}, u32[]{:S(2)}) %collective-permute-start.8) | collective-permute-done | bytes 524320 | tf_op jit(solution)/shard_map/ppermute | solution.py:20
  100.0 11.3 %collective-permute-done.9 = f32[256,512]{1,0:T(8,128)} collective-permute-done((f32[256,512]{1,0:T(8,128)}, f32[256,512]{1,0:T(8,128)}, u32[]{:S(2)}, u32[]{:S(2)}) %collective-permute-start.9) | collective-permute-done | bytes 524320 | tf_op jit(solution)/shard_map/ppermute | solution.py:20
  111.3 5.2 %fusion.36 = f32[256,512]{1,0:T(8,128)} fusion(f32[256,512]{1,0:T(8,128)S(1)} %copy-done.1, f32[256,1024]{1,0:T(8,128)} %all-gather.13.cloned.1.call-done, s32[]{:T(128)S(6)} %select_n.60, f32[256,512]{1,0:T(8,128)} %collective-permute-done.9, f32[256,512]{1,0:T(8,128)} %collective-permute-done.8, f32[256,512]{1,0:T(8,128)S(1)} %collective-permute-done.7, ...), kind=kOutput, calls=%fused_computation.56 | convolution fusion | flops 1614413824 | bytes 4194308 | tf_op jit(solution)/shard_map/dot_general | solution.py:14
  116.5 0.0 all-gather.19.cloned.1.call-update
  116.5 0.2 all-gather.17.cloned.1.call-start
  116.8 1.5 collective-permute-start.10
  118.2 35.4 %collective-permute-done.10 = f32[256,1536]{1,0:T(8,128)S(1)} collective-permute-done((f32[256,1536]{1,0:T(8,128)S(1)}, f32[256,1536]{1,0:T(8,128)S(1)}, u32[]{:S(2)}, u32[]{:S(2)}) %collective-permute-start.10) | collective-permute-done | bytes 1572896 | tf_op jit(solution)/shard_map/ppermute | solution.py:10
  153.6 8.1 %broadcast_select_fusion.1 = (f32[256,1536]{1,0:T(8,128)S(1)}, f32[256,1536]{1,0:T(8,128)S(1)}) fusion(f32[256,1536]{1,0:T(8,128)S(1)} %collective-permute-done.10, pred[]{:T(512)S(6)} %eq.10, f32[256,1024]{1,0:T(8,128)} %all-gather.11.cloned.1.call-done, f32[1,1024,1536]{2,1,0:T(8,128)} %all-gather.21.cloned.1.call-done), kind=kOutput, calls=%fused_computation.58 | convolution fusion | flops 4832624640 | bytes 12058625 | tf_op jit(solution)/shard_map/dot_general | solution.py:14
  161.7 1.9 pad_maximum_fusion
  163.6 0.0 all-gather.17.cloned.1.call-update
  163.6 0.0 all-gather.23.cloned.1.call-start
  163.7 0.7 all-gather.23.cloned.1.call-update
  164.4 6.1 %copy.8 = f32[1,768,1536]{1,2,0:T(8,128)} copy(f32[1,768,1536]{2,1,0:T(8,128)} %param.6) | data formatting | bytes 9437184 | tf_op args[0]
  170.5 6.7 %select_bitcast_fusion.1 = (f32[768,1536]{0,1:T(8,128)}, f32[768,1536]{0,1:T(8,128)}) fusion(f32[1,768,1536]{1,2,0:T(8,128)} %copy.8, pred[]{:T(512)S(6)} %eq.10), kind=kLoop, calls=%fused_computation.4 | loop fusion | flops 2359296 | bytes 14155777 | tf_op jit(solution)/shard_map/jit(_where)/select_n | solution.py:66
  177.3 5.3 %all-gather.19.cloned.1.call-done = f32[2048,512]{1,0:T(8,128)} async-done(((f32[256,512]{1,0:T(8,128)}), f32[2048,512]{1,0:T(8,128)}) %all-gather.19.cloned.1.call-update) | async-done | bytes 4194320 | tf_op jit(solution)/shard_map/all_gather | solution.py:58
  182.5 5.4 %copy.10 = f32[4,2,256,512]{3,1,2,0:T(2,128)S(1)} copy(f32[4,2,256,512]{3,2,1,0:T(8,128)} %bitcast.33) | data formatting | bytes 8388608 | tf_op jit(solution)/shard_map/reshape | solution.py:61
  187.9 3.1 copy.12
  191.0 75.0 %all-gather.17.cloned.1.call-done = f32[1024,3072]{1,0:T(8,128)} async-done(((f32[256,3072]{1,0:T(8,128)}), f32[1024,3072]{1,0:T(8,128)}) %all-gather.17.cloned.1.call-update) | async-done | bytes 12582928 | tf_op jit(solution)/shard_map/all_gather | solution.py:57
  266.0 44.8 %fusion.45 = f32[1024,3072]{1,0:T(8,128)} fusion(f32[1024,1024]{1,0:T(8,128)} %bitcast.34, f32[1024,3072]{1,0:T(8,128)} %all-gather.17.cloned.1.call-done), kind=kOutput, calls=%fused_computation.68 | convolution fusion | flops 38654705664 | bytes 29360128 | tf_op jit(solution)/shard_map/dot_general | solution.py:63
  310.8 1.7 all-gather.23.cloned.1.call-done
  312.5 64.6 %maximum_add_fusion = f32[768,3072]{0,1:T(8,128)} fusion(f32[768,1536]{0,1:T(8,128)} %get-tuple-element.7, f32[768,1536]{0,1:T(8,128)} %get-tuple-element.6, f32[1024,3072]{1,0:T(8,128)} %fusion.45, f32[1,768,1024]{2,1,0:T(8,128)} %all-gather.23.cloned.1.call-done), kind=kOutput, calls=%fused_computation | convolution fusion | flops 28995747840 | bytes 34603008 | tf_op jit(solution)/shard_map/dot_general | solution.py:14
  377.1 14.8 %copy.11 = f32[1,768,2,1536]{3,2,1,0:T(2,128)} copy(f32[1,768,2,1536]{1,3,2,0:T(8,128)} %bitcast.32) | data formatting | bytes 18874368 | tf_op jit(solution)/shard_map/reshape | solution.py:69
  (15 shorter events, 0.0 us)
Async XLA Ops:
  6.5 38.9 %all-gather.11.cloned.1.call-start = ((), (), s32[]{:S(2)}) async-start(), calls=%async_computation | async-start | bytes 1572864 | tf_op jit(solution)/shard_map/all_gather | solution.py:25
  6.5 15.2 %collective-permute-start.3 = (f32[256,512]{1,0:T(8,128)}, f32[256,512]{1,0:T(8,128)S(1)}, u32[]{:S(2)}, u32[]{:S(2)}) collective-permute-start(f32[256,512]{1,0:T(8,128)} %bitcast.36), channel_id=1, source_target_pairs={{0,8},{8,0},{16,24},{24,16},{1,9},{9,1},{17,25},{25,17},{2,10},{10... | collective-permute-start | bytes 1572872 | tf_op jit(solution)/shard_map/ppermute | solution.py:10
  9.6 13.0 %collective-permute-start = (f32[256,512]{1,0:T(8,128)}, f32[256,512]{1,0:T(8,128)S(1)}, u32[]{:S(2)}, u32[]{:S(2)}) collective-permute-start(f32[256,512]{1,0:T(8,128)} %bitcast.37), channel_id=1, source_target_pairs={{0,2},{2,4},{4,6},{6,0},{1,3},{3,5},{5,7},{7,1},{8,10},{10,12},{12... | collective-permute-start | bytes 1572872 | tf_op jit(solution)/shard_map/ppermute | solution.py:20
  21.7 0.8 copy-start.2
  22.5 49.7 %all-gather.15.cloned.1.call-start = ((), (), s32[]{:S(2)}) async-start(), calls=%async_computation.2 | async-start | bytes 1572864 | tf_op jit(solution)/shard_map/all_gather | solution.py:25
  22.6 8.7 %collective-permute-start.1 = (f32[256,512]{1,0:T(8,128)S(1)}, f32[256,512]{1,0:T(8,128)S(1)}, u32[]{:S(2)}, u32[]{:S(2)}) collective-permute-start(f32[256,512]{1,0:T(8,128)S(1)} %collective-permute-done), channel_id=1, source_target_pairs={{0,2},{2,4},{4,6},{6,0},{1,3},{3,5},{5,7},{7,1},{8,10},{10,12},{12... | collective-permute-start | bytes 1572872 | tf_op jit(solution)/shard_map/ppermute | solution.py:20
  31.3 14.1 %collective-permute-start.2 = (f32[256,512]{1,0:T(8,128)S(1)}, f32[256,512]{1,0:T(8,128)S(1)}, u32[]{:S(2)}, u32[]{:S(2)}) collective-permute-start(f32[256,512]{1,0:T(8,128)S(1)} %collective-permute-done.1), channel_id=1, source_target_pairs={{0,2},{2,4},{4,6},{6,0},{1,3},{3,5},{5,7},{7,1},{8,10},{10,12},{12... | collective-permute-start | bytes 1572872 | tf_op jit(solution)/shard_map/ppermute | solution.py:20
  50.8 49.2 %all-gather.13.cloned.1.call-start = ((), (), s32[]{:S(2)}) async-start(), calls=%async_computation.1 | async-start | bytes 1572864 | tf_op jit(solution)/shard_map/all_gather | solution.py:25
  51.5 102.0 %all-gather.21.cloned.1.call-start = ((), (), s32[]{:S(2)}) async-start(), calls=%async_computation.5 | async-start | bytes 7864320 | tf_op jit(solution)/shard_map/all_gather | solution.py:48
  52.1 59.1 %copy-start.1 = (f32[256,512]{1,0:T(8,128)S(1)}, f32[256,512]{1,0:T(8,128)}, u32[]{:S(2)}) copy-start(f32[256,512]{1,0:T(8,128)} %get-tuple-element.10) | copy-start | bytes 1572868
  52.1 130.4 %all-gather.19.cloned.1.call-start = ((), (), s32[]{:S(2)}) async-start(), calls=%async_computation.4 | async-start | bytes 4718592 | tf_op jit(solution)/shard_map/all_gather | solution.py:58
  52.2 8.9 %collective-permute-start.4 = (f32[256,512]{1,0:T(8,128)}, f32[256,512]{1,0:T(8,128)S(1)}, u32[]{:S(2)}, u32[]{:S(2)}) collective-permute-start(f32[256,512]{1,0:T(8,128)} %get-tuple-element.11), channel_id=1, source_target_pairs={{0,2},{2,4},{4,6},{6,0},{1,3},{3,5},{5,7},{7,1},{8,10},{10,12},{12... | collective-permute-start | bytes 1572872 | tf_op jit(solution)/shard_map/ppermute | solution.py:20
  61.1 8.6 %collective-permute-start.5 = (f32[256,512]{1,0:T(8,128)S(1)}, f32[256,512]{1,0:T(8,128)S(1)}, u32[]{:S(2)}, u32[]{:S(2)}) collective-permute-start(f32[256,512]{1,0:T(8,128)S(1)} %collective-permute-done.4), channel_id=1, source_target_pairs={{0,2},{2,4},{4,6},{6,0},{1,3},{3,5},{5,7},{7,1},{8,10},{10,12},{12... | collective-permute-start | bytes 1572872 | tf_op jit(solution)/shard_map/ppermute | solution.py:20
  69.7 8.6 %collective-permute-start.6 = (f32[256,512]{1,0:T(8,128)S(1)}, f32[256,512]{1,0:T(8,128)S(1)}, u32[]{:S(2)}, u32[]{:S(2)}) collective-permute-start(f32[256,512]{1,0:T(8,128)S(1)} %collective-permute-done.5), channel_id=1, source_target_pairs={{0,2},{2,4},{4,6},{6,0},{1,3},{3,5},{5,7},{7,1},{8,10},{10,12},{12... | collective-permute-start | bytes 1572872 | tf_op jit(solution)/shard_map/ppermute | solution.py:20
  82.6 34.2 %copy-start = (f32[1,256,1536]{2,1,0:T(8,128)S(1)}, f32[1,256,1536]{2,1,0:T(8,128)}, u32[]{:S(2)}) copy-start(f32[1,256,1536]{2,1,0:T(8,128)} %param.8) | copy-start | bytes 4718596
  82.6 8.7 %collective-permute-start.7 = (f32[256,512]{1,0:T(8,128)S(1)}, f32[256,512]{1,0:T(8,128)S(1)}, u32[]{:S(2)}, u32[]{:S(2)}) collective-permute-start(f32[256,512]{1,0:T(8,128)S(1)} %fusion.17), channel_id=1, source_target_pairs={{0,2},{2,4},{4,6},{6,0},{1,3},{3,5},{5,7},{7,1},{8,10},{10,12},{12... | collective-permute-start | bytes 1572872 | tf_op jit(solution)/shard_map/ppermute | solution.py:20
  91.3 8.7 %collective-permute-start.8 = (f32[256,512]{1,0:T(8,128)S(1)}, f32[256,512]{1,0:T(8,128)}, u32[]{:S(2)}, u32[]{:S(2)}) collective-permute-start(f32[256,512]{1,0:T(8,128)S(1)} %collective-permute-done.7), channel_id=1, source_target_pairs={{0,2},{2,4},{4,6},{6,0},{1,3},{3,5},{5,7},{7,1},{8,10},{10,12},{12... | collective-permute-start | bytes 1572872 | tf_op jit(solution)/shard_map/ppermute | solution.py:20
  100.0 11.3 %collective-permute-start.9 = (f32[256,512]{1,0:T(8,128)}, f32[256,512]{1,0:T(8,128)}, u32[]{:S(2)}, u32[]{:S(2)}) collective-permute-start(f32[256,512]{1,0:T(8,128)} %collective-permute-done.8), channel_id=1, source_target_pairs={{0,2},{2,4},{4,6},{6,0},{1,3},{3,5},{5,7},{7,1},{8,10},{10,12},{12... | collective-permute-start | bytes 1572872 | tf_op jit(solution)/shard_map/ppermute | solution.py:20
  116.5 149.5 %all-gather.17.cloned.1.call-start = ((), (), s32[]{:S(2)}) async-start(), calls=%async_computation.3 | async-start | bytes 15728640 | tf_op jit(solution)/shard_map/all_gather | solution.py:57
  116.8 36.8 %collective-permute-start.10 = (f32[256,1536]{1,0:T(8,128)S(1)}, f32[256,1536]{1,0:T(8,128)S(1)}, u32[]{:S(2)}, u32[]{:S(2)}) collective-permute-start(f32[256,1536]{1,0:T(8,128)S(1)} %bitcast.35), channel_id=1, source_target_pairs={{0,8},{8,0},{16,24},{24,16},{1,9},{9,1},{17,25},{25,17},{2,10},{10... | collective-permute-start | bytes 4718600 | tf_op jit(solution)/shard_map/ppermute | solution.py:10
  163.6 148.9 %all-gather.23.cloned.1.call-start = ((), (), s32[]{:S(2)}) async-start(), calls=%async_computation.6 | async-start | bytes 4718592 | tf_op jit(solution)/shard_map/all_gather | solution.py:68
Sparse Core Ops, SparseCore 0:
  22.7 22.6 all-gather.10
  50.9 21.2 all-gather.14
  73.8 21.2 all-gather.12
  96.5 47.6 all-gather.20
  145.9 36.5 all-gather.18
  183.9 82.0 all-gather.16
  267.6 44.8 all-gather.22
